TPU v7x, 32 devices: a whole 2x2x4 slice. The times are simulated.
32 devices in a mesh: groups: 2 (over x), wide: 16 (over z, y, core).
Axes of the slice: x: 2, y: 2, z: 4, core: 2. Of those that a mesh axis runs over, the one named last changes fastest.
Arguments:
- frames_in: bfloat16 [128, 256, 768], P(('groups', 'wide')), parts along dimension 0, may hold values from -5 to 5
- qkv_spatial: bfloat16 [768, 2304], replicated, may hold values from -6.5 to 6.5
- out_spatial: bfloat16 [768, 768], replicated, may hold values from -0.21875 to 0.21875
- qkv_temporal: bfloat16 [768, 2304], replicated, may hold values from -6.5 to 6.5
- out_temporal: bfloat16 [768, 768], replicated, may hold values from -0.21875 to 0.21875
Outputs:
- frames_out: bfloat16 [128, 256, 768], P(('groups', 'wide')), parts along dimension 0
There are 2 independent parts, one for each index of `groups`. A program takes and returns all parts, laid end to end along the dimension named above; an argument that names none is the same for every part. Nothing has to cross between parts.
All inputs are finite; a program needn't handle non-finite values.
Results may differ from a plain program's by a relative error of at most 0.008.
Values may be sent and summed in bfloat16 or wider, within the bound.
A program may use at most 128 MiB of HBM per device.

v0:
```python
import jax
import jax.numpy as jnp
from jax import lax
from jax.sharding import PartitionSpec as P

HEADS = 12
HEAD_DIM = 64


def normalize(tensor):
    floats = tensor.astype(jnp.float32)
    average = jnp.mean(floats, axis=-1, keepdims=True)
    centred = floats - average
    spread = jnp.mean(centred * centred, axis=-1, keepdims=True)
    return (centred * lax.rsqrt(spread + 1e-06)).astype(jnp.bfloat16)


def project(flat_rows, matrix):
    return jnp.dot(flat_rows, matrix, preferred_element_type=jnp.float32)


def attend(projected, score_form, mix_form):
    leading = projected.shape[:-1]
    split = projected.reshape(leading + (3, HEADS, HEAD_DIM))
    queries = split[..., 0, :, :]
    key_part = split[..., 1, :, :]
    values = split[..., 2, :, :]
    scores = jnp.einsum(
        score_form, queries, key_part, preferred_element_type=jnp.float32
    ) * HEAD_DIM ** (-0.5)
    weights = jax.nn.softmax(scores, axis=-1).astype(jnp.bfloat16)
    mixed = jnp.einsum(mix_form, weights, values, preferred_element_type=jnp.float32)
    return mixed.reshape(leading + (HEADS * HEAD_DIM,)).astype(jnp.bfloat16)


def attend_time(received):
    frame_total, single, item_count, columns = received.shape
    sequences = received.reshape(frame_total, item_count, columns)
    result = attend(sequences, "qbhd,kbhd->bhqk", "bhqk,kbhd->qbhd")
    return result.reshape(frame_total, single, item_count, HEADS * HEAD_DIM)


def shards(frames_in, qkv_spatial, out_spatial, qkv_temporal, out_temporal):
    frame_count, patch_count, features = frames_in.shape
    wide_count = lax.axis_size("wide")
    per_group = patch_count // wide_count
    first = normalize(frames_in)
    proj_one = project(first.reshape(-1, features), qkv_spatial).astype(jnp.bfloat16)
    proj_one = proj_one.reshape(frame_count, patch_count, 3 * features)
    spatial = attend(proj_one, "bqhd,bkhd->bhqk", "bhqk,bkhd->bqhd")
    update = project(spatial.reshape(-1, features), out_spatial).reshape(
        frame_count, patch_count, features
    )
    middle = (frames_in.astype(jnp.float32) + update).astype(jnp.bfloat16)
    second = normalize(middle)
    grouped = second.reshape(frame_count, wide_count, per_group, features)
    received = lax.all_to_all(grouped, "wide", split_axis=1, concat_axis=0, tiled=True)
    frame_total, single, item_count, columns = received.shape
    local_proj = project(received.reshape(-1, columns), qkv_temporal).astype(jnp.bfloat16)
    local_proj = local_proj.reshape(frame_total, single, item_count, 3 * columns)
    temporal = attend_time(local_proj)
    returned = lax.all_to_all(temporal, "wide", split_axis=0, concat_axis=1, tiled=True)
    change = project(returned.reshape(-1, features), out_temporal).reshape(
        frame_count, patch_count, features
    )
    return (middle.astype(jnp.float32) + change).astype(jnp.bfloat16)


def solution(mesh):
    return jax.shard_map(
        shards,
        mesh=mesh,
        in_specs=(P(("groups", "wide"), None, None), P(), P(), P(), P()),
        out_specs=P(("groups", "wide"), None, None),
        check_vma=False,
    )
```

profile of v0, /device:TPU:1, one launch (start us, length us, event | category | flops | bytes accessed | tf_op | source)
XLA Modules:
  0.0 206.3 jit_solution(2839607701515157252)
XLA Ops:
  0.0 1.8 convert_reduce_fusion.1
  1.9 2.1 %fusion.16 = f32[4,256]{1,0:T(4,128)S(1)} fusion(bf16[4,256,768]{2,1,0:T(8,128)(2,1)} %param.5, f32[4,256]{1,0:T(4,128)S(1)} %broadcast_multiply_fusion.1), kind=kLoop, calls=%fused_computation.26 | loop fusion | flops 3144704 | bytes 1581056 | tf_op jit(solution)/shard_map/reduce_sum | solution.py:14
  4.0 0.4 fusion.17
  4.5 0.0 copy-done
  4.5 5.5 %convolution_convert_fusion.1 = bf16[1024,2304]{1,0:T(8,128)(2,1)} fusion(bf16[1024,768]{1,0:T(8,128)(2,1)S(1)} %bitcast.56, bf16[768,2304]{1,0:T(8,128)(2,1)S(1)} %copy-done), kind=kOutput, calls=%fused_computation.11 | convolution fusion | flops 3626237952 | bytes 9830400 | tf_op jit(solution)/shard_map/dot_general | solution.py:19
  10.0 6.6 %copy.29 = bf16[1024,2304]{0,1:T(8,128)(2,1)} copy(bf16[1024,2304]{1,0:T(8,128)(2,1)} %convolution_convert_fusion.1) | data formatting | bytes 9437184 | tf_op jit(solution)/shard_map/convert_element_type | solution.py:48
  16.6 8.9 %reshape_reshape.3 = bf16[4,256,3,12,64]{1,0,4,3,2:T(4,128)(2,1)} reshape(bf16[1024,2304]{0,1:T(8,128)(2,1)} %copy.29) | data formatting | bytes 9437184 | tf_op jit(solution)/shard_map/reshape;reshape | solution.py:24
  25.5 3.3 %fusion.35 = (bf16[4,256,1,12,64]{1,0,4,3,2:T(4,128)(2,1)S(1)}, bf16[4,256,1,12,64]{1,0,4,3,2:T(4,128)(2,1)S(1)}, bf16[4,256,1,12,64]{1,0,4,3,2:T(4,128)(2,1)S(1)}) fusion(bf16[4,256,3,12,64]{1,0,4,3,2:T(4,128)(2,1)} %reshape_reshape.3), kind=kLoop, calls=%fused_computation.52 | loop fusion | bytes 9437184 | tf_op jit(solution)/shard_map/slice | solution.py:27
  28.9 6.4 %fusion.29 = f32[4,12,256,256]{2,3,1,0:T(8,128)} fusion(bf16[4,256,1,12,64]{1,0,4,3,2:T(4,128)(2,1)S(1)} %get-tuple-element.10, bf16[4,256,1,12,64]{1,0,4,3,2:T(4,128)(2,1)S(1)} %get-tuple-element.9), kind=kOutput, calls=%fused_computation.40 | convolution fusion | flops 402653184 | bytes 15728640 | tf_op jit(solution)/shard_map/bqhd,bkhd->bhqk/dot_general | solution.py:28
  35.3 15.8 %fusion.36 = (f32[4,12,256]{2,1,0:T(8,128)S(1)}, f32[4,12,256,256]{2,3,1,0:T(8,128)}) fusion(f32[4,12,256,256]{2,3,1,0:T(8,128)} %fusion.29), kind=kOutput, calls=%fused_computation.53 | output fusion | flops 12583167 | bytes 25214976 | tf_op jit(solution)/shard_map/sub | solution.py:31
  51.1 5.8 %fusion.28 = bf16[4,12,64,256]{3,2,1,0:T(8,128)(2,1)S(1)} fusion(f32[4,12,256,256]{2,3,1,0:T(8,128)} %get-tuple-element.12, f32[4,12,256]{2,1,0:T(8,128)S(1)} %get-tuple-element.11, bf16[4,256,1,12,64]{1,0,4,3,2:T(4,128)(2,1)S(1)} %get-tuple-element.8), kind=kOutput, calls=%fused_computation.38 | convolution fusion | flops 409731072 | bytes 15777792 | tf_op jit(solution)/shard_map/bhqk,bkhd->bqhd/dot_general | solution.py:32
  56.9 1.6 convert_reduce_fusion
  58.5 0.6 fusion.14
  59.1 0.4 fusion.15
  59.5 0.0 copy-start.6
  59.6 0.2 copy.35
  59.7 43.9 %all_to_all.30 = bf16[4,16,16,768]{3,2,0,1:T(8,128)(2,1)S(1)} all-to-all(bf16[4,16,16,768]{3,2,0,1:T(8,128)(2,1)S(1)} %copy.35), channel_id=1, replica_groups=mesh['groups'=2,'wide'=16] {'wide'}, dimensions={1} | all-to-all | bytes 3145728 | tf_op jit(solution)/shard_map/all_to_all | solution.py:57
  103.6 5.4 %convolution_convert_fusion = bf16[1024,2304]{1,0:T(8,128)(2,1)} fusion(bf16[1024,768]{1,0:T(8,128)(2,1)S(1)} %bitcast.58, bf16[768,2304]{1,0:T(8,128)(2,1)S(1)} %copy-done.6), kind=kOutput, calls=%fused_computation.10 | convolution fusion | flops 3626237952 | bytes 9830400 | tf_op jit(solution)/shard_map/dot_general | solution.py:19
  109.0 14.9 %reshape_reshape_reshape.3 = bf16[64,16,3,12,64]{4,3,2,1,0:T(8,128)(2,1)} reshape(bf16[1024,2304]{1,0:T(8,128)(2,1)} %convolution_convert_fusion) | data formatting | bytes 9437184 | tf_op jit(solution)/shard_map/reshape;reshape;reshape | solution.py:24
  124.0 9.2 %fusion.34 = (bf16[64,16,1,12,64]{4,3,2,1,0:T(8,128)(2,1)}, bf16[64,16,1,12,64]{4,3,2,1,0:T(8,128)(2,1)}, bf16[64,16,1,12,64]{4,3,2,1,0:T(8,128)(2,1)}) fusion(bf16[64,16,3,12,64]{4,3,2,1,0:T(8,128)(2,1)} %reshape_reshape_reshape.3), kind=kLoop, calls=%fused_computation.51 | loop fusion | bytes 9437184 | tf_op jit(solution)/shard_map/slice | solution.py:27
  133.2 6.4 %copy.48 = bf16[64,16,1,12,64]{0,4,3,1,2:T(8,128)(2,1)S(1)} copy(bf16[64,16,1,12,64]{4,3,2,1,0:T(8,128)(2,1)} %get-tuple-element.5) | data formatting | bytes 3145728
  139.7 7.2 %fusion.21 = f32[16,12,64,64]{2,3,1,0:T(8,128)S(1)} fusion(bf16[64,16,1,12,64]{4,3,2,1,0:T(8,128)(2,1)} %get-tuple-element.6, bf16[64,16,1,12,64]{4,3,2,1,0:T(8,128)(2,1)} %get-tuple-element.7), kind=kOutput, calls=%fused_computation.32 | convolution fusion | flops 100663296 | bytes 6291456 | tf_op jit(solution)/shard_map/qbhd,kbhd->bhqk/dot_general | solution.py:28
  146.9 9.2 %fusion.37 = (f32[16,12,64]{2,1,0:T(8,128)S(1)}, f32[16,12,64,64]{2,3,1,0:T(8,128)S(1)}) fusion(f32[16,12,64,64]{2,3,1,0:T(8,128)S(1)} %fusion.21), kind=kOutput, calls=%fused_computation.54 | output fusion | flops 3145791 | bytes 6340608 | tf_op jit(solution)/shard_map/sub | solution.py:31
  156.0 2.6 %fusion.25 = bf16[16,12,64,64]{3,2,1,0:T(8,128)(2,1)} fusion(f32[16,12,64,64]{2,3,1,0:T(8,128)S(1)} %get-tuple-element.16, f32[16,12,64]{2,1,0:T(8,128)S(1)} %get-tuple-element.15, bf16[64,16,1,12,64]{0,4,3,1,2:T(8,128)(2,1)S(1)} %copy.48), kind=kOutput, calls=%fused_computation.37 | convolution fusion | flops 103022592 | bytes 6340608 | tf_op jit(solution)/shard_map/bhqk,kbhd->qbhd/dot_general | solution.py:32
  158.7 3.9 %copy.40 = bf16[64,1,16,768]{3,2,1,0:T(8,128)(2,1)S(1)} copy(bf16[64,1,16,768]{0,3,2,1:T(8,128)(2,1)} %bitcast.55) | data formatting | bytes 3145728 | tf_op jit(solution)/shard_map/convert_element_type | solution.py:33
  162.6 0.0 copy-start.5
  162.6 0.0 copy-start.8
  162.6 41.0 %all_to_all.31 = bf16[64,1,16,768]{3,2,1,0:T(8,128)(2,1)S(1)} all-to-all(bf16[64,1,16,768]{3,2,1,0:T(8,128)(2,1)S(1)} %copy.40), channel_id=1, replica_groups=mesh['groups'=2,'wide'=16] {'wide'}, dimensions={0} | all-to-all | bytes 3145728 | tf_op jit(solution)/shard_map/all_to_all | solution.py:62
  203.6 0.1 copy.41
  203.8 0.0 copy-start.1
  203.8 0.0 copy-done.5
  203.8 2.5 %fusion.19 = bf16[4,256,768]{2,1,0:T(8,128)(2,1)} fusion(bf16[4,256,768]{2,1,0:T(8,128)(2,1)S(1)} %copy-done.5, bf16[4,256,768]{2,1,0:T(8,128)(2,1)S(1)} %bitcast.57, bf16[768,768]{1,0:T(8,128)(2,1)S(1)} %copy-done.8), kind=kOutput, calls=%fused_computation.29 | convolution fusion | flops 1210318848 | bytes 5898240 | tf_op jit(solution)/shard_map/dot_general | solution.py:19
  (16 shorter events, 0.1 us)
Async XLA Ops:
  0.0 4.5 %copy-start = (bf16[768,2304]{1,0:T(8,128)(2,1)S(1)}, bf16[768,2304]{1,0:T(8,128)(2,1)}, u32[]{:S(2)}) copy-start(bf16[768,2304]{1,0:T(8,128)(2,1)} %param.6) | copy-start | bytes 10616836
  0.0 4.0 %copy-start.2 = (bf16[4,256,768]{2,1,0:T(8,128)(2,1)S(1)}, bf16[4,256,768]{2,1,0:T(8,128)(2,1)}, u32[]{:S(2)}) copy-start(bf16[4,256,768]{2,1,0:T(8,128)(2,1)} %param.5) | copy-start | bytes 4718596
  51.1 5.8 %copy-start.3 = (bf16[4,256,768]{2,1,0:T(8,128)(2,1)S(1)}, bf16[4,256,768]{2,1,0:T(8,128)(2,1)}, u32[]{:S(2)}) copy-start(bf16[4,256,768]{2,1,0:T(8,128)(2,1)} %param.5) | copy-start | bytes 4718596
  51.1 5.8 %copy-start.7 = (bf16[768,768]{1,0:T(8,128)(2,1)S(1)}, bf16[768,768]{1,0:T(8,128)(2,1)}, u32[]{:S(2)}) copy-start(bf16[768,768]{1,0:T(8,128)(2,1)} %param.7) | copy-start | bytes 3538948
  58.5 1.2 copy-start.4
  59.5 44.1 %copy-start.6 = (bf16[768,2304]{1,0:T(8,128)(2,1)S(1)}, bf16[768,2304]{1,0:T(8,128)(2,1)}, u32[]{:S(2)}) copy-start(bf16[768,2304]{1,0:T(8,128)(2,1)} %param.8) | copy-start | bytes 10616836
  162.6 41.2 %copy-start.5 = (bf16[4,256,768]{2,1,0:T(8,128)(2,1)S(1)}, bf16[4,256,768]{2,1,0:T(8,128)(2,1)}, u32[]{:S(2)}) copy-start(bf16[4,256,768]{2,1,0:T(8,128)(2,1)} %copy-done.4) | copy-start | bytes 4718596
  162.6 41.2 %copy-start.8 = (bf16[768,768]{1,0:T(8,128)(2,1)S(1)}, bf16[768,768]{1,0:T(8,128)(2,1)}, u32[]{:S(2)}) copy-start(bf16[768,768]{1,0:T(8,128)(2,1)} %param.9) | copy-start | bytes 3538948
  203.8 2.6 %copy-start.1 = (bf16[768,2304]{1,0:T(8,128)(2,1)S(1)}, bf16[768,2304]{1,0:T(8,128)(2,1)}, u32[]{:S(2)}) copy-start(bf16[768,2304]{1,0:T(8,128)(2,1)} %param.6) | copy-start | bytes 10616836
where the time goes:
time: 207 us; the launch traced here: 206 us
  blocking collectives  84.9 us (41%)
  local copies, waits for them, and re-layouts  53.7 us (26%)
  matrix products  37.1 us (18%)
  other arithmetic  30.4 us (15%)
    all_to_all x1, blocking collectives, shards(): lax.all_to_all(grouped, 'wide', split_axis=1, concat_axis=0, tiled=True)  43.9 us
    all_to_all x1, blocking collectives, shards(): lax.all_to_all(temporal, 'wide', split_axis=0, concat_axis=1, tiled=True)  41 us
    sub x2, other arithmetic, attend(): weights = jax.nn.softmax(scores, axis=-1).astype(jnp.bfloat16)  24.9 us
    another operation x2, local copies, waits for them, and re-layouts, attend(): split = projected.reshape(leading + (3, HEADS, HEAD_DIM))  23.9 us
    dot_general x4, matrix products, project(): return jnp.dot(flat_rows, matrix, preferred_element_type=jnp.float32)  15.1 us
    dot_general x2, matrix products, attend(): jnp.einsum(score_form, queries, key_part, preferred_element_type=jnp.floa...  13.6 us
    slice x2, local copies, waits for them, and re-layouts, attend(): values = split[..., 2, :, :]  12.6 us
    dot_general x2, matrix products, attend(): jnp.einsum(mix_form, weights, values, preferred_element_type=jnp.float32)  8.47 us

commit v1 on v0

--- a/solution.py
+++ b/solution.py
@@ -59,7 +59,10 @@
     local_proj = project(received.reshape(-1, columns), qkv_temporal).astype(jnp.bfloat16)
     local_proj = local_proj.reshape(frame_total, single, item_count, 3 * columns)
     temporal = attend_time(local_proj)
-    returned = lax.all_to_all(temporal, "wide", split_axis=0, concat_axis=1, tiled=True)
+    n_dev = lax.axis_size("wide")
+    shards_2 = jnp.stack(jnp.split(temporal, n_dev, axis=0), axis=0)
+    shards_2 = lax.all_to_all(shards_2, "wide", split_axis=0, concat_axis=0)
+    returned = jnp.concatenate(shards_2, axis=1)
     change = project(returned.reshape(-1, features), out_temporal).reshape(
         frame_count, patch_count, features
     )

time: 207 us -> 199 us (0.961)
  local copies, waits for them, and re-layouts: 53.7 us -> 49.1 us
  matrix products: 37.1 us -> 34.7 us
    unnamed x19 -> x57, local copies, waits for them, and re-layouts: 6.49 us -> 2.21 us
    split x0 -> x17, local copies, waits for them, and re-layouts: none -> 4.17 us  [shards(): shards_2 = jnp.stack(jnp.split(temporal, n_dev, axis=0), axis=0)]
    convert_element_type x1 -> x0, local copies, waits for them, and re-layouts: 3.89 us -> none  [attend(): return mixed.reshape(leading + (HEADS * HEAD_DIM,)).astype(jnp.bfloat16)]
    dot_general x2, matrix products: 13.6 us -> 10.1 us  [attend(): jnp.einsum(score_form, queries, key_part, preferred_element_type=jnp.floa...]
    slice x2, local copies, waits for them, and re-layouts: 12.6 us -> 9.24 us  [attend(): values = split[..., 2, :, :]]
    another operation x0 -> x17, local copies, waits for them, and re-layouts: none -> 2.67 us  [shards(): shards_2 = jnp.stack(jnp.split(temporal, n_dev, axis=0), axis=0)]
where the time goes in v1:
time: 199 us; the launch traced here: 198 us
  blocking collectives  84.7 us (43%)
  local copies, waits for them, and re-layouts  49.1 us (25%)
  matrix products  34.7 us (17%)
  other arithmetic  29.1 us (15%)
    all_to_all x1, blocking collectives, shards(): lax.all_to_all(grouped, 'wide', split_axis=1, concat_axis=0, tiled=True)  43.9 us
    all_to_all x1, blocking collectives, shards(): shards_2 = lax.all_to_all(shards_2, 'wide', split_axis=0, concat_axis=0)  40.8 us
    sub x2, other arithmetic, attend(): weights = jax.nn.softmax(scores, axis=-1).astype(jnp.bfloat16)  25.1 us
    another operation x2, local copies, waits for them, and re-layouts, attend(): split = projected.reshape(leading + (3, HEADS, HEAD_DIM))  23.8 us
    dot_general x4, matrix products, project(): return jnp.dot(flat_rows, matrix, preferred_element_type=jnp.float32)  15 us
    dot_general x2, matrix products, attend(): jnp.einsum(score_form, queries, key_part, preferred_element_type=jnp.floa...  10.1 us
    dot_general x2, matrix products, attend(): jnp.einsum(mix_form, weights, values, preferred_element_type=jnp.float32)  9.57 us
    slice x2, local copies, waits for them, and re-layouts, attend(): values = split[..., 2, :, :]  9.24 us

profile of v1, /device:TPU:1, one launch (start us, length us, event | category | flops | bytes accessed | tf_op | source)
XLA Modules:
  0.0 198.1 jit_solution(14481359140444804451)
XLA Ops:
  0.0 1.8 convert_reduce_fusion.1
  1.9 0.2 copy-done.2
  2.0 0.6 fusion.16
  2.6 0.4 fusion.17
  3.1 5.5 %convolution_convert_fusion.1 = bf16[1024,2304]{1,0:T(8,128)(2,1)} fusion(bf16[1024,768]{1,0:T(8,128)(2,1)S(1)} %bitcast.52, bf16[768,2304]{1,0:T(8,128)(2,1)S(1)} %copy-done), kind=kOutput, calls=%fused_computation.11 | convolution fusion | flops 3626237952 | bytes 9830400 | tf_op jit(solution)/shard_map/dot_general | solution.py:19
  8.6 6.6 %copy.15 = bf16[1024,2304]{0,1:T(8,128)(2,1)} copy(bf16[1024,2304]{1,0:T(8,128)(2,1)} %convolution_convert_fusion.1) | data formatting | bytes 9437184 | tf_op jit(solution)/shard_map/convert_element_type | solution.py:48
  15.3 8.9 %reshape_reshape.4 = bf16[4,256,3,12,64]{1,0,4,3,2:T(4,128)(2,1)} reshape(bf16[1024,2304]{0,1:T(8,128)(2,1)} %copy.15) | data formatting | bytes 9437184 | tf_op jit(solution)/shard_map/reshape;reshape | solution.py:24
  24.2 3.3 %fusion.31 = (bf16[4,256,1,12,64]{1,0,4,3,2:T(4,128)(2,1)S(1)}, bf16[4,256,1,12,64]{1,0,4,3,2:T(4,128)(2,1)S(1)}, bf16[4,256,1,12,64]{1,0,4,3,2:T(4,128)(2,1)S(1)}) fusion(bf16[4,256,3,12,64]{1,0,4,3,2:T(4,128)(2,1)} %reshape_reshape.4), kind=kLoop, calls=%fused_computation.68 | loop fusion | bytes 9437184 | tf_op jit(solution)/shard_map/slice | solution.py:27
  27.5 6.4 %fusion.25 = f32[4,12,256,256]{2,3,1,0:T(8,128)} fusion(bf16[4,256,1,12,64]{1,0,4,3,2:T(4,128)(2,1)S(1)} %get-tuple-element.10, bf16[4,256,1,12,64]{1,0,4,3,2:T(4,128)(2,1)S(1)} %get-tuple-element.9), kind=kOutput, calls=%fused_computation.40 | convolution fusion | flops 402653184 | bytes 15728640 | tf_op jit(solution)/shard_map/bqhd,bkhd->bhqk/dot_general | solution.py:28
  33.9 15.8 %fusion.33 = (f32[4,12,256]{2,1,0:T(8,128)S(1)}, f32[4,12,256,256]{2,3,1,0:T(8,128)}) fusion(f32[4,12,256,256]{2,3,1,0:T(8,128)} %fusion.25), kind=kOutput, calls=%fused_computation.70 | output fusion | flops 12583167 | bytes 25214976 | tf_op jit(solution)/shard_map/sub | solution.py:31
  49.7 5.8 %fusion.24 = bf16[4,12,64,256]{3,2,1,0:T(8,128)(2,1)S(1)} fusion(f32[4,12,256,256]{2,3,1,0:T(8,128)} %get-tuple-element.28, f32[4,12,256]{2,1,0:T(8,128)S(1)} %get-tuple-element.27, bf16[4,256,1,12,64]{1,0,4,3,2:T(4,128)(2,1)S(1)} %get-tuple-element.8), kind=kOutput, calls=%fused_computation.38 | convolution fusion | flops 409731072 | bytes 15777792 | tf_op jit(solution)/shard_map/bhqk,bkhd->bqhd/dot_general | solution.py:32
  55.5 1.6 convert_reduce_fusion
  57.1 0.6 fusion.14
  57.7 0.4 fusion.15
  58.2 0.2 copy.21
  58.4 43.9 %all_to_all.20 = bf16[4,16,16,768]{3,2,0,1:T(8,128)(2,1)S(1)} all-to-all(bf16[4,16,16,768]{3,2,0,1:T(8,128)(2,1)S(1)} %copy.21), channel_id=1, replica_groups=mesh['groups'=2,'wide'=16] {'wide'}, dimensions={1} | all-to-all | bytes 3145728 | tf_op jit(solution)/shard_map/all_to_all | solution.py:57
  102.3 5.4 %convolution_convert_fusion = bf16[1024,2304]{1,0:T(8,128)(2,1)} fusion(bf16[1024,768]{1,0:T(8,128)(2,1)S(1)} %bitcast.54, bf16[768,2304]{1,0:T(8,128)(2,1)S(1)} %copy-done.18), kind=kOutput, calls=%fused_computation.10 | convolution fusion | flops 3626237952 | bytes 9830400 | tf_op jit(solution)/shard_map/dot_general | solution.py:19
  107.7 14.9 %reshape_reshape_reshape.3 = bf16[64,16,3,12,64]{4,3,2,1,0:T(8,128)(2,1)} reshape(bf16[1024,2304]{1,0:T(8,128)(2,1)} %convolution_convert_fusion) | data formatting | bytes 9437184 | tf_op jit(solution)/shard_map/reshape;reshape;reshape | solution.py:24
  122.6 5.9 %fusion.30 = (bf16[64,16,1,12,64]{4,3,2,1,0:T(8,128)(2,1)S(1)}, bf16[64,16,1,12,64]{4,3,2,1,0:T(8,128)(2,1)S(1)}, bf16[64,16,1,12,64]{4,3,2,1,0:T(8,128)(2,1)S(1)}) fusion(bf16[64,16,3,12,64]{4,3,2,1,0:T(8,128)(2,1)} %reshape_reshape_reshape.3), kind=kLoop, calls=%fused_computation.67 | loop fusion | bytes 9437184 | tf_op jit(solution)/shard_map/slice | solution.py:27
  128.5 3.7 %fusion.21 = f32[16,12,64,64]{2,3,1,0:T(8,128)S(1)} fusion(bf16[64,16,1,12,64]{4,3,2,1,0:T(8,128)(2,1)S(1)} %get-tuple-element.7, bf16[64,16,1,12,64]{4,3,2,1,0:T(8,128)(2,1)S(1)} %get-tuple-element.6), kind=kOutput, calls=%fused_computation.32 | convolution fusion | flops 100663296 | bytes 6291456 | tf_op jit(solution)/shard_map/qbhd,kbhd->bhqk/dot_general | solution.py:28
  132.3 9.4 %fusion.34 = (f32[16,12,64]{2,1,0:T(8,128)S(1)}, f32[16,12,64,64]{2,3,1,0:T(8,128)S(1)}) fusion(f32[16,12,64,64]{2,3,1,0:T(8,128)S(1)} %fusion.21), kind=kOutput, calls=%fused_computation.71 | output fusion | flops 3145791 | bytes 6340608 | tf_op jit(solution)/shard_map/sub | solution.py:31
  141.7 3.7 %convert_bitcast_fusion = bf16[64,16,12,64]{3,0,2,1:T(8,128)(2,1)S(1)} fusion(f32[16,12,64,64]{2,3,1,0:T(8,128)S(1)} %get-tuple-element.32, f32[16,12,64]{2,1,0:T(8,128)S(1)} %get-tuple-element.31, bf16[64,16,1,12,64]{4,3,2,1,0:T(8,128)(2,1)S(1)} %get-tuple-element.5), kind=kOutput, calls=%fused_computation.35 | convolution fusion | flops 103022592 | bytes 6340608 | tf_op jit(solution)/shard_map/bhqk,kbhd->qbhd/dot_general | solution.py:32
  145.4 2.5 %fusion.32 = (bf16[4,16,12,64]{3,0,2,1:T(4,128)(2,1)S(1)}, bf16[4,16,12,64]{3,0,2,1:T(4,128)(2,1)}, bf16[4,16,12,64]{3,0,2,1:T(4,128)(2,1)}, bf16[4,16,12,64]{3,...) fusion(bf16[64,16,12,64]{3,0,2,1:T(8,128)(2,1)S(1)} %convert_bi, ...), kind=kLoop, calls=%fused_computation.69 | loop fusion | bytes 3145728 | tf_op jit(solution)/shard_map/split | solution.py:63
  147.9 0.2 stack.66
  148.1 1.0 copy.40
  149.2 0.2 stack.65
  149.4 0.2 stack.64
  149.9 0.2 stack.62
  153.0 40.8 %all_to_all.21 = bf16[16,4,1,16,768]{4,3,1,2,0:T(8,128)(2,1)S(1)} all-to-all(bf16[16,4,1,16,768]{4,3,1,2,0:T(8,128)(2,1)S(1)} %constant_dynamic-update-slice_fusion), channel_id=1, replica_groups=mesh['groups'=2,'wide'=16] {'wide'}, dimensions={0} | all-to-all | bytes 3145728 | tf_op jit(solution)/shard_map/all_to_all | solution.py:64
  193.9 1.3 copy-done.5
  195.2 0.3 copy-done.20
  195.5 2.5 %fusion.19 = bf16[4,256,768]{2,1,0:T(8,128)(2,1)} fusion(bf16[4,256,768]{2,1,0:T(8,128)(2,1)S(1)} %copy-done.5, bf16[4,256,768]{2,1,0:T(8,128)(2,1)S(1)} %bitcast.53, bf16[768,768]{1,0:T(8,128)(2,1)S(1)} %copy-done.20), kind=kOutput, calls=%fused_computation.29 | convolution fusion | flops 1210318848 | bytes 5898240 | tf_op jit(solution)/shard_map/dot_general | solution.py:19
  (87 shorter events, 3.2 us)
Async XLA Ops:
  0.0 3.1 %copy-start = (bf16[768,2304]{1,0:T(8,128)(2,1)S(1)}, bf16[768,2304]{1,0:T(8,128)(2,1)}, u32[]{:S(2)}) copy-start(bf16[768,2304]{1,0:T(8,128)(2,1)} %param.6) | copy-start | bytes 10616836
  0.0 2.0 %copy-start.2 = (bf16[4,256,768]{2,1,0:T(8,128)(2,1)S(1)}, bf16[4,256,768]{2,1,0:T(8,128)(2,1)}, u32[]{:S(2)}) copy-start(bf16[4,256,768]{2,1,0:T(8,128)(2,1)} %param.5) | copy-start | bytes 4718596
  49.7 5.8 %copy-start.3 = (bf16[4,256,768]{2,1,0:T(8,128)(2,1)S(1)}, bf16[4,256,768]{2,1,0:T(8,128)(2,1)}, u32[]{:S(2)}) copy-start(bf16[4,256,768]{2,1,0:T(8,128)(2,1)} %param.5) | copy-start | bytes 4718596
  49.7 5.8 %copy-start.19 = (bf16[768,768]{1,0:T(8,128)(2,1)S(1)}, bf16[768,768]{1,0:T(8,128)(2,1)}, u32[]{:S(2)}) copy-start(bf16[768,768]{1,0:T(8,128)(2,1)} %param.7) | copy-start | bytes 3538948
  57.1 1.1 copy-start.4
  58.2 44.1 %copy-start.18 = (bf16[768,2304]{1,0:T(8,128)(2,1)S(1)}, bf16[768,2304]{1,0:T(8,128)(2,1)}, u32[]{:S(2)}) copy-start(bf16[768,2304]{1,0:T(8,128)(2,1)} %param.8) | copy-start | bytes 10616836
  147.9 1.4 copy-start.17
  147.9 1.7 copy-start.16
  147.9 1.9 copy-start.15
  148.1 1.9 copy-start.14
  149.3 1.0 copy-start.13
  149.6 1.0 copy-start.12
  149.8 1.0 copy-start.11
  150.1 1.0 copy-start.10
  150.3 1.0 copy-start.9
  150.6 1.0 copy-start.8
  150.8 1.0 copy-start.7
  151.1 1.0 copy-start.6
  193.8 1.4 copy-start.5
  193.8 1.7 copy-start.20
  195.5 2.6 %copy-start.1 = (bf16[768,2304]{1,0:T(8,128)(2,1)S(1)}, bf16[768,2304]{1,0:T(8,128)(2,1)}, u32[]{:S(2)}) copy-start(bf16[768,2304]{1,0:T(8,128)(2,1)} %param.6) | copy-start | bytes 10616836
